TPU v7x, 512 devices: a whole 4x4x16 slice. The times are simulated.
512 devices in a mesh: row: 16 (over z), col: 32 (over x, y, core).
Axes of the slice: x: 4, y: 4, z: 16, core: 2. Of those that a mesh axis runs over, the one named last changes fastest.
Arguments:
- gate_pre: bfloat16 [2048, 16384], P('row', 'col'), may hold values from -6 to 6
- up_pre: bfloat16 [2048, 16384], P('row', 'col'), may hold values from -6 to 6
- down_weight: bfloat16 [8192, 16384], P('row', 'col'), may hold values from -0.125 to 0.125
- block_mask: int32 [64, 128], P('row', 'col'), may hold values from 0 to 1, as said below
- cotangent: bfloat16 [2048, 8192], P('row', 'col'), may hold values from -6 to 6
Outputs:
- output: bfloat16 [2048, 8192], P('row', 'col')
- d_gate: bfloat16 [2048, 16384], P('row', 'col')
- d_up: bfloat16 [2048, 16384], P('row', 'col')
- d_down: bfloat16 [8192, 16384], P('row', 'col')
Inputs may be any that keep to these rules, and one draw needn't show every extreme that they name: `block_mask`: each device's tile of 4 x 4 blocks keeps between 4 and 12 blocks; in every draw some tile keeps exactly 12.
All inputs are finite; a program needn't handle non-finite values.
Results may differ from a plain program's by a relative error of at most 0.015.
Values may be sent and summed in bfloat16 or wider, within the bound.
A program may use at most 64 MiB of HBM per device.

v0:
```python
import jax
import jax.numpy as jnp
from jax import lax
from jax.sharding import PartitionSpec as P


def rounded_f32(values):
    return lax.optimization_barrier(values.astype(jnp.bfloat16)).astype(jnp.float32)


def body(gate_pre, up_pre, down_weight, block_mask, cotangent):
    tok_rows, ff_cols = gate_pre.shape
    d_rows = down_weight.shape[0]
    tile_r, tile_c = block_mask.shape
    block_size = d_rows // tile_r
    gate_wide = gate_pre.astype(jnp.float32)
    up_wide = up_pre.astype(jnp.float32)
    activated = jax.nn.silu(gate_wide)
    hidden = (activated * up_wide).astype(jnp.bfloat16)
    expand = jnp.repeat(jnp.repeat(block_mask, block_size, axis=0), block_size, axis=1)
    masked = jnp.where(expand > 0, down_weight, jnp.zeros_like(down_weight))
    cot_row = lax.all_gather(cotangent, "col", axis=1, tiled=True)
    cot_all = lax.all_to_all(cot_row, "row", split_axis=1, concat_axis=0, tiled=True)
    panel = lax.all_gather(masked, "row", axis=0, tiled=True)
    columns = lax.dot_general(
        hidden, panel, (((1,), (1,)), ((), ())), preferred_element_type=jnp.float32
    )
    y_partial = columns
    shards = panel.shape[0] // d_rows
    per_shard = jnp.einsum(
        "tnd,ndf->ntf",
        cot_row.reshape(tok_rows, shards, d_rows),
        panel.reshape(shards, d_rows, ff_cols),
        preferred_element_type=jnp.float32,
    )
    d_hidden = jnp.sum(rounded_f32(per_shard), axis=0)
    y_partial, d_hidden = (y_partial, d_hidden)
    y_summand = rounded_f32(y_partial)
    hidden_all = lax.all_gather(hidden, "row", axis=0, tiled=True)
    grad_full = lax.dot_general(
        cot_all, hidden_all, (((0,), (0,)), ((), ())), preferred_element_type=jnp.float32
    )
    output = lax.psum_scatter(
        y_summand.astype(jnp.bfloat16), "col", scatter_dimension=1, tiled=True
    )
    sigmoid_g = jax.nn.sigmoid(gate_wide)
    d_gate = (d_hidden * up_wide * sigmoid_g * (1.0 + gate_wide * (1.0 - sigmoid_g))).astype(
        jnp.bfloat16
    )
    d_up = (d_hidden * activated).astype(jnp.bfloat16)
    d_down = jnp.where(expand > 0, grad_full, jnp.zeros_like(grad_full)).astype(jnp.bfloat16)
    return (output, d_gate, d_up, d_down)


def solution(mesh):
    in_specs = (P("row", "col"), P("row", "col"), P("row", "col"), P("row", "col"), P("row", "col"))
    out_specs = (P("row", "col"), P("row", "col"), P("row", "col"), P("row", "col"))
    return jax.shard_map(body, mesh=mesh, in_specs=in_specs, out_specs=out_specs, check_vma=False)
```

profile of v0, /device:TPU:2, one launch (start us, length us, event | category | flops | bytes accessed | tf_op | source)
XLA Modules:
  0.0 470.4 jit_solution(9010206070040514916)
XLA Ops:
  7.2 0.0 all-gather.6.cloned.1.call-start
  7.2 1.6 copy.32
  8.9 0.0 all-gather.6.cloned.1.call-update
  8.9 0.0 all-gather.4.cloned.1.call-start
  8.9 0.7 broadcast_compare_fusion
  9.6 0.1 copy.29
  9.7 0.1 broadcast_bitcast_fusion
  9.8 1.3 copy.30
  11.1 0.8 bitcast_select_fusion.1
  11.9 0.0 all-gather.4.cloned.1.call-update
  12.0 0.1 copy.27
  12.1 0.1 copy.28
  12.2 62.5 %all-gather.6.cloned.1.call-done = bf16[128,8192]{0,1:T(8,128)(2,1)} async-done(((bf16[128,256]{0,1:T(8,128)(2,1)}), bf16[128,8192]{0,1:T(8,128)(2,1)}) %all-gather.6.cloned.1.call-update) | async-done | bytes 2097168 | tf_op jit(solution)/shard_map/all_gather | solution.py:22
  74.7 12.3 %all-to-all-start = ((bf16[128,16,512]{0,2,1:T(8,128)(2,1)}), bf16[128,16,512]{0,2,1:T(8,128)(2,1)S(1)}, u32[]{:S(2)}, u32[]{:S(2)}) async-start(bf16[128,16,512]{0,2,1:T(8,128)(2,1)} %bitcast.33), calls=%async_computation.1 | async-start | bytes 4194304 | tf_op jit(solution)/shard_map/all_to_all | solution.py:23
  87.0 0.0 all-gather.8.cloned.1.call-start
  87.1 179.0 %all-gather.4.cloned.1.call-done = bf16[8192,512]{0,1:T(8,128)(2,1)} async-done(((bf16[512,512]{0,1:T(8,128)(2,1)}), bf16[8192,512]{0,1:T(8,128)(2,1)}) %all-gather.4.cloned.1.call-update) | async-done | bytes 8388624 | tf_op jit(solution)/shard_map/all_gather | solution.py:24
  266.1 11.9 %copy.31 = bf16[8192,512]{1,0:T(8,128)(2,1)} copy(bf16[8192,512]{0,1:T(8,128)(2,1)} %all-gather.4.cloned.1.call-done) | data formatting | bytes 16777216 | tf_op jit(solution)/shard_map/all_gather | solution.py:24
  277.9 6.5 %convert_bitcast_fusion = bf16[16,128,512]{1,2,0:T(8,128)(2,1)S(1)} fusion(bf16[16,512,512]{2,1,0:T(8,128)(2,1)} %bitcast.30, bf16[128,16,512]{0,2,1:T(8,128)(2,1)} %bitcast.34), kind=kOutput, calls=%fused_computation.2 | convolution fusion | flops 1074790400 | bytes 12582912 | tf_op jit(solution)/shard_map/tnd,ndf->ntf/dot_general | solution.py:30
  284.4 0.3 convert_reduce_fusion
  284.7 0.8 multiply_convert_fusion
  285.6 0.0 all-gather.8.cloned.1.call-update
  285.6 0.0 reduce-scatter.2.cloned.1.call-start
  285.6 6.1 %convolution_convert_fusion = bf16[128,8192]{1,0:T(8,128)(2,1)} fusion(bf16[128,512]{0,1:T(8,128)(2,1)} %get-tuple-element.22, bf16[8192,512]{0,1:T(8,128)(2,1)} %all-gather.4.cloned.1.call-done), kind=kOutput, calls=%fused_computation | convolution fusion | flops 1074790400 | bytes 10616832 | tf_op jit(solution)/shard_map/dot_general | solution.py:25
  291.8 0.0 reduce-scatter.2.cloned.1.call-update
  291.8 0.0 all-to-all-done
  291.8 2.6 copy.35
  294.4 0.8 copy.36
  295.2 0.8 copy.37
  296.0 65.9 %all-gather.8.cloned.1.call-done = bf16[2048,512]{0,1:T(8,128)(2,1)} async-done(((bf16[128,512]{0,1:T(8,128)(2,1)}), bf16[2048,512]{0,1:T(8,128)(2,1)}) %all-gather.8.cloned.1.call-update) | async-done | bytes 2097168 | tf_op jit(solution)/shard_map/all_gather | solution.py:39
  361.9 3.5 fusion
  365.3 1.0 copy.38
  366.4 97.6 %reduce-scatter.2.cloned.1.call-done = bf16[128,256]{1,0:T(8,128)(2,1)} async-done(((bf16[128,8192]{1,0:T(8,128)(2,1)}), bf16[128,256]{1,0:T(8,128)(2,1)}) %reduce-scatter.2.cloned.1.call-update) | async-done | bytes 65552 | tf_op jit(solution)/shard_map/reduce_scatter | solution.py:43
  (5 shorter events, 0.0 us)
Async XLA Ops:
  7.2 4.8 %copy-start = (bf16[128,512]{1,0:T(8,128)(2,1)S(1)}, bf16[128,512]{1,0:T(8,128)(2,1)}, u32[]{:S(2)}) copy-start(bf16[128,512]{1,0:T(8,128)(2,1)} %param.5) | copy-start | bytes 393220
  7.2 4.9 %copy-start.1 = (bf16[128,512]{1,0:T(8,128)(2,1)S(1)}, bf16[128,512]{1,0:T(8,128)(2,1)}, u32[]{:S(2)}) copy-start(bf16[128,512]{1,0:T(8,128)(2,1)} %param.6) | copy-start | bytes 393220
  7.2 67.5 %all-gather.6.cloned.1.call-start = ((), (), s32[]{:S(2)}) async-start(), calls=%async_computation.4 | async-start | bytes 2162688 | tf_op jit(solution)/shard_map/all_gather | solution.py:22
  8.9 257.2 %all-gather.4.cloned.1.call-start = ((), (), s32[]{:S(2)}) async-start(), calls=%async_computation.2 | async-start | bytes 8912896 | tf_op jit(solution)/shard_map/all_gather | solution.py:24
  74.7 217.1 %all-to-all-start = ((bf16[128,16,512]{0,2,1:T(8,128)(2,1)}), bf16[128,16,512]{0,2,1:T(8,128)(2,1)S(1)}, u32[]{:S(2)}, u32[]{:S(2)}) async-start(bf16[128,16,512]{0,2,1:T(8,128)(2,1)} %bitcast.33), calls=%async_computation.1 | async-start | bytes 4194304 | tf_op jit(solution)/shard_map/all_to_all | solution.py:23
  87.0 274.9 %all-gather.8.cloned.1.call-start = ((), (), s32[]{:S(2)}) async-start(), calls=%async_computation.5 | async-start | bytes 2228224 | tf_op jit(solution)/shard_map/all_gather | solution.py:39
  285.6 178.3 %reduce-scatter.2.cloned.1.call-start = ((), (), s32[]{:S(2)}) async-start(), calls=%async_computation.3 | async-start | bytes 2162688 | tf_op jit(solution)/shard_map/reduce_scatter | solution.py:43
Sparse Core Ops, SparseCore 0:
  11.7 62.9 all-gather.5
  77.4 188.6 all-gather.3
  285.7 76.1 all-gather.7
  366.7 97.1 reduce-scatter.1
where the time goes:
time: 471 us; the launch traced here: 470 us
  waiting for transfers between devices  405 us (86%)
  local copies, waits for them, and re-layouts  20.3 us (4%)
  matrix products  16.1 us (3%)
  between operations  13.8 us (3%)
  starting transfers between devices  12.4 us (3%)
    all_gather x1, waiting for transfers between devices, body(): panel = lax.all_gather(masked, 'row', axis=0, tiled=True)  179 us
    reduce_scatter x1, waiting for transfers between devices, body(): lax.psum_scatter(y_summand.astype(jnp.bfloat16), 'col', scatter_dimension...  97.6 us
    all_gather x1, waiting for transfers between devices, body(): hidden_all = lax.all_gather(hidden, 'row', axis=0, tiled=True)  65.9 us
    all_gather x1, waiting for transfers between devices, body(): cot_row = lax.all_gather(cotangent, 'col', axis=1, tiled=True)  62.5 us
    all_to_all x1, starting transfers between devices, body(): lax.all_to_all(cot_row, 'row', split_axis=1, concat_axis=0, tiled=True)  12.3 us
    all_gather x1, local copies, waits for them, and re-layouts, body(): panel = lax.all_gather(masked, 'row', axis=0, tiled=True)  11.9 us
  transfers between devices with their start and end apart: 5, of which 4 were waited for; matrix products, arithmetic and copies ran while one was open for 8% of the time, Pallas kernels for 0%

commit v1 on v0

--- a/solution.py
+++ b/solution.py
@@ -19,7 +19,17 @@
     hidden = (activated * up_wide).astype(jnp.bfloat16)
     expand = jnp.repeat(jnp.repeat(block_mask, block_size, axis=0), block_size, axis=1)
     masked = jnp.where(expand > 0, down_weight, jnp.zeros_like(down_weight))
-    cot_row = lax.all_gather(cotangent, "col", axis=1, tiled=True)
+
+    def _plan_loads(block_in):
+        column = []
+        for _ in range(lax.axis_size("col")):
+            column.append(block_in)
+        shaped = jnp.concatenate(
+            lax.all_to_all(jnp.stack(column), axis_name="col", split_axis=0, concat_axis=0), axis=1
+        )
+        return shaped
+
+    cot_row = _plan_loads(cotangent)
     cot_all = lax.all_to_all(cot_row, "row", split_axis=1, concat_axis=0, tiled=True)
     panel = lax.all_gather(masked, "row", axis=0, tiled=True)
     columns = lax.dot_general(

time: 471 us -> 417 us (0.89)
  waiting for transfers between devices: 405 us -> 340 us
  starting transfers between devices: 12.4 us -> 23.1 us
    all_gather x1 -> x0, waiting for transfers between devices: 62.5 us -> none  [body(): cot_row = lax.all_gather(cotangent, 'col', axis=1, tiled=True)]
    all_gather x1, waiting for transfers between devices: 179 us -> 150 us  [body(): panel = lax.all_gather(masked, 'row', axis=0, tiled=True)]
    all_to_all x0 -> x1, waiting for transfers between devices: none -> 25.7 us  [_plan_loads(): lax.all_to_all(jnp.stack(column), axis_name='col', split_axis=0, concat_a...]
    all_to_all x0 -> x1, starting transfers between devices: none -> 10.4 us  [_plan_loads(): lax.all_to_all(jnp.stack(column), axis_name='col', split_axis=0, concat_a...]
  transfers between devices with their start and end apart: 5 -> 5, of which waited for: 4 -> 4; matrix products, arithmetic and copies ran while one was open for 8% -> 9% of each run, Pallas kernels for 0% -> 0%
where the time goes in v1:
time: 417 us; the launch traced here: 416 us
  waiting for transfers between devices  340 us (82%)
  starting transfers between devices  23.1 us (6%)
  local copies, waits for them, and re-layouts  20.7 us (5%)
  matrix products  16.1 us (4%)
  between operations  13.8 us (3%)
    all_gather x1, waiting for transfers between devices, body(): panel = lax.all_gather(masked, 'row', axis=0, tiled=True)  150 us
    reduce_scatter x1, waiting for transfers between devices, body(): lax.psum_scatter(y_summand.astype(jnp.bfloat16), 'col', scatter_dimension...  97.7 us
    all_gather x1, waiting for transfers between devices, body(): hidden_all = lax.all_gather(hidden, 'row', axis=0, tiled=True)  67 us
    all_to_all x1, waiting for transfers between devices, _plan_loads(): lax.all_to_all(jnp.stack(column), axis_name='col', split_axis=0, concat_a...  25.7 us
    all_to_all x1, starting transfers between devices, body(): lax.all_to_all(cot_row, 'row', split_axis=1, concat_axis=0, tiled=True)  12.6 us
    all_gather x1, local copies, waits for them, and re-layouts, body(): panel = lax.all_gather(masked, 'row', axis=0, tiled=True)  11.9 us
    all_to_all x1, starting transfers between devices, _plan_loads(): lax.all_to_all(jnp.stack(column), axis_name='col', split_axis=0, concat_a...  10.4 us
  transfers between devices with their start and end apart: 5, of which 4 were waited for; matrix products, arithmetic and copies ran while one was open for 9% of the time, Pallas kernels for 0%

profile of v1, /device:TPU:2, one launch (start us, length us, event | category | flops | bytes accessed | tf_op | source)
XLA Modules:
  0.0 416.4 jit_solution(968516433331875145)
XLA Ops:
  7.2 0.0 all-gather.3.cloned.1.call-start
  7.2 0.7 broadcast_compare_fusion
  7.9 0.1 copy.29
  8.0 0.1 broadcast_bitcast_fusion
  8.1 1.3 copy.30
  9.4 0.8 bitcast_select_fusion.1
  10.2 0.0 all-gather.3.cloned.1.call-update
  10.2 0.1 copy.32
  10.4 1.9 stack.2
  12.2 10.4 %all-to-all-start = ((bf16[32,128,256]{1,2,0:T(8,128)(2,1)}), bf16[32,128,256]{1,2,0:T(8,128)(2,1)}, u32[]{:S(2)}, u32[]{:S(2)}) async-start(bf16[32,128,256]{1,2,0:T(8,128)(2,1)} %stack.2), calls=%async_computation.1 | async-start | bytes 4194304 | tf_op jit(solution)/shard_map/all_to_all | solution.py:28
  22.6 0.1 copy.27
  22.8 0.1 copy.28
  22.9 25.7 %all-to-all-done = bf16[32,128,256]{1,2,0:T(8,128)(2,1)} async-done(((bf16[32,128,256]{1,2,0:T(8,128)(2,1)}), bf16[32,128,256]{1,2,0:T(8,128)(2,1)}, u32[]{:S(2)}, u32[]{:S(2)}) %all-to-all-start) | async-done | bytes 2097184 | tf_op jit(solution)/shard_map/all_to_all | solution.py:28
  48.6 12.6 %all-to-all-start.1 = ((bf16[128,16,512]{0,2,1:T(8,128)(2,1)}), bf16[128,16,512]{0,2,1:T(8,128)(2,1)S(1)}, u32[]{:S(2)}, u32[]{:S(2)}) async-start(bf16[128,16,512]{0,2,1:T(8,128)(2,1)} %bitcast.3), calls=%async_computation.2 | async-start | bytes 4194304 | tf_op jit(solution)/shard_map/all_to_all | solution.py:33
  61.2 0.0 all-gather.5.cloned.1.call-start
  61.2 149.7 %all-gather.3.cloned.1.call-done = bf16[8192,512]{0,1:T(8,128)(2,1)} async-done(((bf16[512,512]{0,1:T(8,128)(2,1)}), bf16[8192,512]{0,1:T(8,128)(2,1)}) %all-gather.3.cloned.1.call-update) | async-done | bytes 8388624 | tf_op jit(solution)/shard_map/all_gather | solution.py:34
  210.9 11.9 %copy.31 = bf16[8192,512]{1,0:T(8,128)(2,1)} copy(bf16[8192,512]{0,1:T(8,128)(2,1)} %all-gather.3.cloned.1.call-done) | data formatting | bytes 16777216 | tf_op jit(solution)/shard_map/all_gather | solution.py:34
  222.8 6.5 %convert_bitcast_fusion = bf16[16,128,512]{1,2,0:T(8,128)(2,1)S(1)} fusion(bf16[16,512,512]{2,1,0:T(8,128)(2,1)} %bitcast.32, bf16[128,16,512]{0,2,1:T(8,128)(2,1)} %bitcast.3), kind=kOutput, calls=%fused_computation.2 | convolution fusion | flops 1074790400 | bytes 12582912 | tf_op jit(solution)/shard_map/tnd,ndf->ntf/dot_general | solution.py:40
  229.3 0.3 convert_reduce_fusion
  229.6 0.8 multiply_convert_fusion
  230.4 0.0 all-gather.5.cloned.1.call-update
  230.4 0.0 reduce-scatter.2.cloned.1.call-start
  230.5 6.1 %convolution_convert_fusion = bf16[128,8192]{1,0:T(8,128)(2,1)} fusion(bf16[128,512]{0,1:T(8,128)(2,1)} %get-tuple-element.22, bf16[8192,512]{0,1:T(8,128)(2,1)} %all-gather.3.cloned.1.call-done), kind=kOutput, calls=%fused_computation | convolution fusion | flops 1074790400 | bytes 10616832 | tf_op jit(solution)/shard_map/dot_general | solution.py:35
  236.6 0.0 reduce-scatter.2.cloned.1.call-update
  236.6 0.0 all-to-all-done.1
  236.6 2.6 copy.35
  239.2 0.8 copy.36
  240.0 0.8 copy.37
  240.8 67.0 %all-gather.5.cloned.1.call-done = bf16[2048,512]{0,1:T(8,128)(2,1)} async-done(((bf16[128,512]{0,1:T(8,128)(2,1)}), bf16[2048,512]{0,1:T(8,128)(2,1)}) %all-gather.5.cloned.1.call-update) | async-done | bytes 2097168 | tf_op jit(solution)/shard_map/all_gather | solution.py:49
  307.8 3.5 fusion
  311.2 1.0 copy.38
  312.2 97.7 %reduce-scatter.2.cloned.1.call-done = bf16[128,256]{1,0:T(8,128)(2,1)} async-done(((bf16[128,8192]{1,0:T(8,128)(2,1)}), bf16[128,256]{1,0:T(8,128)(2,1)}) %reduce-scatter.2.cloned.1.call-update) | async-done | bytes 65552 | tf_op jit(solution)/shard_map/reduce_scatter | solution.py:53
  (7 shorter events, 0.0 us)
Async XLA Ops:
  7.2 3.1 copy-start.2
  7.2 203.7 %all-gather.3.cloned.1.call-start = ((), (), s32[]{:S(2)}) async-start(), calls=%async_computation.3 | async-start | bytes 8912896 | tf_op jit(solution)/shard_map/all_gather | solution.py:34
  12.2 10.4 %copy-start = (bf16[128,512]{1,0:T(8,128)(2,1)S(1)}, bf16[128,512]{1,0:T(8,128)(2,1)}, u32[]{:S(2)}) copy-start(bf16[128,512]{1,0:T(8,128)(2,1)} %param.5) | copy-start | bytes 393220
  12.2 10.5 %copy-start.1 = (bf16[128,512]{1,0:T(8,128)(2,1)S(1)}, bf16[128,512]{1,0:T(8,128)(2,1)}, u32[]{:S(2)}) copy-start(bf16[128,512]{1,0:T(8,128)(2,1)} %param.6) | copy-start | bytes 393220
  12.2 36.4 %all-to-all-start = ((bf16[32,128,256]{1,2,0:T(8,128)(2,1)}), bf16[32,128,256]{1,2,0:T(8,128)(2,1)}, u32[]{:S(2)}, u32[]{:S(2)}) async-start(bf16[32,128,256]{1,2,0:T(8,128)(2,1)} %stack.2), calls=%async_computation.1 | async-start | bytes 4194304 | tf_op jit(solution)/shard_map/all_to_all | solution.py:28
  48.6 188.0 %all-to-all-start.1 = ((bf16[128,16,512]{0,2,1:T(8,128)(2,1)}), bf16[128,16,512]{0,2,1:T(8,128)(2,1)S(1)}, u32[]{:S(2)}, u32[]{:S(2)}) async-start(bf16[128,16,512]{0,2,1:T(8,128)(2,1)} %bitcast.3), calls=%async_computation.2 | async-start | bytes 4194304 | tf_op jit(solution)/shard_map/all_to_all | solution.py:33
  61.2 246.6 %all-gather.5.cloned.1.call-start = ((), (), s32[]{:S(2)}) async-start(), calls=%async_computation.5 | async-start | bytes 2228224 | tf_op jit(solution)/shard_map/all_gather | solution.py:49
  230.4 179.5 %reduce-scatter.2.cloned.1.call-start = ((), (), s32[]{:S(2)}) async-start(), calls=%async_computation.4 | async-start | bytes 2162688 | tf_op jit(solution)/shard_map/reduce_scatter | solution.py:53
Sparse Core Ops, SparseCore 0:
  10.6 200.2 all-gather.2
  230.5 77.1 all-gather.4
  312.8 97.1 reduce-scatter.1
